TPU v7x, 256 devices: a whole 4x4x8 slice. The times are simulated.
256 devices in a mesh: tm: 8 (over z), lat: 4 (over x), lon: 8 (over y, core).
Axes of the slice: x: 4, y: 4, z: 8, core: 2. Of those that a mesh axis runs over, the one named last changes fastest.
Arguments:
- slab: bfloat16 [512, 262144], P('tm', ('lat', 'lon')), may hold values from -6 to 6
- start: bfloat16 [512, 64], P('tm'), may hold values from -6 to 6
- sections: float32 [3, 2], replicated, may hold values from 0.2 to 1.5708, as said below
Outputs:
- basis: float32 [2048, 64, 128], P(('lat', 'lon', 'tm'))
- pcs: float32 [512, 64], P('tm')
Inputs may be any that keep to these rules, and one draw needn't show every extreme that they name: `sections`: in each column, one section has radius 0.78 to 0.86 and angle 2 pi / 8 to 2 pi / 4, the other radius 0.9955 to 0.9985 and angle 2 pi / 24 to 2 pi / 12; which column is which varies; amplitudes 0.2 to 1.0.
All inputs are finite; a program needn't handle non-finite values.
Results may differ from a plain program's by a relative error of at most 0.0039.
Values may be sent and summed in bfloat16 or wider, within the bound.
A program may use at most 64 MiB of HBM per device.

v0:
```python
import math
import jax
import jax.numpy as jnp
from jax import lax
from jax.sharding import PartitionSpec as P

LANES = 128
TOP_PRECISION = lax.Precision.HIGHEST


def prefix(value, axis, join, neutral):
    count, mine = (lax.axis_size(axis), lax.axis_index(axis))
    pieces = jax.tree.map(lambda part: lax.all_gather(part, axis), value)
    running = jax.tree.map(
        lambda part, zero: jnp.full_like(part, 0) + jnp.asarray(zero, part.dtype), value, neutral
    )

    def step(position, running):
        longer = join(running, jax.tree.map(lambda part: part[position], pieces))
        return jax.tree.map(lambda new, old: jnp.where(position < mine, new, old), longer, running)

    return lax.fori_loop(0, count - 1, step, running)


def impulse(radius, angle, steps):
    counted = jnp.maximum(steps, 0).astype(jnp.float32)
    values = jnp.exp(counted * jnp.log(radius)) * jnp.sin((counted + 1.0) * angle) / jnp.sin(angle)
    return jnp.where(steps >= 0, values, 0.0)


def section_columns(radius, angle, feed_two, drive_gain, times):
    return [
        -drive_gain * impulse(radius, angle, times - 1),
        -drive_gain * impulse(radius, angle, times),
        impulse(radius, angle, times + 1),
        feed_two * impulse(radius, angle, times),
    ]


def block_maps(sections, hour_count):
    radius = sections[0]
    angles = sections[1]
    amplitude = sections[2]
    feed_two = -radius * radius
    drive_gain = amplitude * jnp.sqrt(1.0 - radius * radius)
    hours = jnp.arange(hour_count, dtype=jnp.int32)
    lag = hours[:, None] - hours[None, :]
    drive_rows = jnp.zeros((hour_count, hour_count), jnp.float32)
    input_rows = [
        (hours == hour_count - 1).astype(jnp.float32),
        (hours == hour_count - 2).astype(jnp.float32),
    ]
    state_parts = []
    end_rows = [jnp.zeros((6,), jnp.float32), jnp.zeros((6,), jnp.float32)]
    for section in range(2):
        rad = radius[section]
        ang = angles[section]
        drive_rows = drive_rows + drive_gain[section] * (
            impulse(rad, ang, lag) - impulse(rad, ang, lag - 2)
        )
        for back in range(2):
            ahead = hour_count - 1 - back - hours
            input_rows.append(
                drive_gain[section] * (impulse(rad, ang, ahead) - impulse(rad, ang, ahead - 2))
            )
        state_parts.append(section_columns(rad, ang, feed_two[section], drive_gain[section], hours))
        for back in range(2):
            moment = jnp.array(hour_count - 1 - back, jnp.int32)
            pieces = section_columns(rad, ang, feed_two[section], drive_gain[section], moment)
            zeros_pair = [jnp.zeros((), jnp.float32), jnp.zeros((), jnp.float32)]
            own = pieces[2:] + zeros_pair if section == 0 else zeros_pair + pieces[2:]
            end_rows.append(jnp.stack(pieces[:2] + own))
    first, second = state_parts
    state_rows = jnp.stack(
        [first[0] + second[0], first[1] + second[1], first[2], first[3], second[2], second[3]],
        axis=1,
    )
    end_inputs = jnp.stack(input_rows)
    end_state = jnp.stack(end_rows)
    return (drive_rows, end_inputs, state_rows, end_state)


def combine(earlier, subsequent):
    concatenated_rows = jnp.dot(subsequent[0], earlier[0], precision=TOP_PRECISION)
    vector = jnp.dot(subsequent[0], earlier[1], precision=TOP_PRECISION) + subsequent[1]
    return (concatenated_rows, vector)


def make_orthonormal(spatial_patterns):
    local_gram_block = jnp.einsum(
        "zrs,zts->rt", spatial_patterns, spatial_patterns, precision=TOP_PRECISION
    )
    gram_matrix = lax.psum(local_gram_block, ("tm", "lat", "lon"))
    lower_factor = jnp.linalg.cholesky(gram_matrix)
    width = gram_matrix.shape[0]
    inverse_factor = jax.scipy.linalg.solve_triangular(
        lower_factor, jnp.eye(width, dtype=jnp.float32), lower=True
    )
    return jnp.einsum("de,wes->wds", inverse_factor, spatial_patterns, precision=TOP_PRECISION)


def local(slab, start, sections):
    hour_count, cell_count = slab.shape
    width = start.shape[1]
    drive_rows, end_inputs, state_rows, end_state = block_maps(sections, hour_count)
    values = slab.astype(jnp.float32)
    local_part = jnp.dot(drive_rows, values, precision=TOP_PRECISION)
    leaving = jnp.dot(end_inputs, values, precision=TOP_PRECISION)
    identity_pair = (jnp.eye(6, dtype=jnp.float32), jnp.zeros_like(leaving))
    entering = prefix((end_state, leaving), "tm", combine, identity_pair)[1]
    filtered = (local_part + jnp.dot(state_rows, entering, precision=TOP_PRECISION)).astype(
        jnp.bfloat16
    )
    grouped = filtered.reshape(hour_count, cell_count // LANES, LANES)
    cells_all = cell_count * lax.axis_size("lat") * lax.axis_size("lon")
    hours_all = hour_count * lax.axis_size("tm")
    block_of_rows = grouped
    spatial_patterns = lax.psum_scatter(
        jnp.einsum("tk,tgc->gkc", start, block_of_rows, preferred_element_type=jnp.float32),
        "tm",
        scatter_dimension=0,
        tiled=True,
    )
    ortho = make_orthonormal(spatial_patterns)
    block_of_rows = grouped.astype(jnp.float32)
    partial_sums = jnp.zeros((hour_count, width), jnp.float32) + jnp.einsum(
        "tgc,gkc->tk",
        block_of_rows,
        lax.all_gather(ortho.astype(jnp.bfloat16), "tm", axis=0, tiled=True).astype(jnp.float32),
        precision=TOP_PRECISION,
    )
    projections = lax.psum(partial_sums, ("lat", "lon"))
    basis = ortho * math.sqrt(cells_all)
    pcs = projections * math.sqrt(hours_all / cells_all)
    return (basis, pcs)


def solution(mesh):
    return jax.shard_map(
        local,
        mesh=mesh,
        in_specs=(P("tm", ("lat", "lon")), P("tm", None), P()),
        out_specs=(P(("lat", "lon", "tm"), None, None), P("tm", None)),
        check_vma=False,
    )
```

profile of v0, /device:TPU:32, one launch (start us, length us, event | category | flops | bytes accessed | tf_op | source)
XLA Modules:
  0.0 378.2 jit_solution(5782166197295645485)
XLA Ops:
  7.2 1.0 slice_reduce_fusion
  8.2 1.5 fusion.87
  9.7 0.7 fusion.89
  13.1 1.4 fusion.80
  14.5 1.4 fusion.79
  15.9 1.2 convolution_bitcast_fusion
  20.7 0.7 fusion.88
  28.4 1.3 compare_select_fusion.9
  29.7 1.9 multiply_add_fusion.1
  31.7 1.3 compare_select_fusion.8
  33.0 27.4 %all-gather.2 = f32[8,6,6]{2,1,0:T(8,128)S(1)} all-gather(f32[1,6,6]{2,1,0:T(8,128)S(1)} %bitcast.79), channel_id=2, replica_groups=mesh['tm'=8,'lat'=4,'lon'=8] {'tm'}, dimensions={0}, use_global_device_ids=true | all-gather | bytes 1296 | tf_op jit(solution)/shard_map/all_gather | solution.py:13
  60.5 9.5 %while.14 = (s32[]{:T(128)}, f32[6,8192]{1,0:T(8,128)S(1)}, s32[]{:T(128)}, f32[8,6,6]{2,1,0:T(8,128)S(1)}, f32[8,6,8192]{2,1,0:T(8,128)}, /*index=5*/s32[]{:T(128)}, s32[]{:T(128)}) while((s32[]{:T(128)}, f32[6,8192]{1,0:T(8,128)S(1)}, s32[]{:T(128)}, f32[8,6,6]{2,1,0:T(8,128)S(1)}, f32[8,6,8192]{2,1,0:T(8,128)}, ...), condition=%wide.region_1.2_spmd.clone, body=%wide.region_0.1_spmd.clone.sunk | while | flops 3735556 | bytes 1317479 | solution.py:22
  60.5 1.3 fusion.106
  61.9 1.3 fusion.106
  63.3 1.3 fusion.106
  64.6 1.3 fusion.106
  66.0 1.3 fusion.106
  67.4 1.3 fusion.106
  68.7 1.3 fusion.106
  70.0 1.8 fusion.90
  71.9 4.2 %fusion.9 = bf16[8,64,8,128]{3,2,1,0:T(8,128)(2,1)S(1)} fusion(f32[64,8192]{1,0:T(8,128)S(1)} %fusion.90, bf16[64,8192]{1,0:T(8,128)(2,1)S(1)} %copy-done, f32[]{:T(128)S(6)} %sin.238, f32[]{:T(128)} %bitcast.5, f32[]{:T(128)} %bitcast.4, f32[]{:T(128)} %bitcast.3, f32[]{:T(128)S(6)} %sin.235, f32[]{:T(128)} %bitcast.2, f32[]{:T(128)} %bitcast.1, f32[]{:T(128)} %bitcast), kind=kOutput, calls=%fused_computation.13 | convolution fusion | flops 403845120 | bytes 4194336 | tf_op jit(solution)/shard_map/dot_general | solution.py:107
  76.1 1.8 convolution_bitcast_fusion.1
  78.0 42.0 %reduce-scatter.2.cloned.1.call-done = f32[8,64,128]{2,1,0:T(8,128)} async-done(((f32[64,64,128]{2,1,0:T(8,128)}), f32[8,64,128]{2,1,0:T(8,128)}) %reduce-scatter.2.cloned.1.call-update) | async-done | bytes 262160 | tf_op jit(solution)/shard_map/reduce_scatter | solution.py:118
  120.0 1.4 convolution_bitcast_fusion.4
  121.4 74.9 %psum.14 = f32[64,64]{0,1:T(8,128)S(1)} all-reduce(f32[64,64]{0,1:T(8,128)S(1)} %convolution_bitcast_fusion.4), channel_id=1, replica_groups=mesh['tm'=8,'lat'=4,'lon'=8] {'tm','lat','lon'}, use_global_device_ids=true, to_apply=%region_3.4 | all-reduce | flops 4096 | bytes 32768 | tf_op jit(solution)/shard_map/psum | solution.py:93
  196.5 5.8 %cholesky.16 = f32[64,64]{1,0:T(8,128)S(1)} custom-call(f32[64,64]{1,0:T(8,128)S(1)} %fusion.16), custom_call_target="Cholesky" | custom-call | tf_op jit(solution)/shard_map/jit(cholesky)/cholesky | solution.py:94
  203.0 0.7 fusion.14
  203.6 4.9 %custom-call.7 = f32[1,64,64]{1,2,0:T(8,128)S(1)} custom-call(f32[1,64,64]{2,1,0:T(8,128)S(1)} %fusion.14), custom_call_target="InvertDiagBlocksLowerTriangular" | custom-call | tf_op jit(solution)/shard_map/jit(_solve_triangular)/triangular_solve | solution.py:96
  208.8 2.1 convert_bitcast_fusion
  210.9 34.8 %all-gather.7.cloned.1.call-done = bf16[64,64,128]{2,1,0:T(8,128)(2,1)} async-done(((bf16[8,64,128]{2,1,0:T(8,128)(2,1)}), bf16[64,64,128]{2,1,0:T(8,128)(2,1)}) %all-gather.7.cloned.1.call-update) | async-done | bytes 1048592 | tf_op jit(solution)/shard_map/all_gather | solution.py:129
  245.6 1.6 convolution_bitcast_fusion.2
  247.3 123.8 %psum.15 = f32[64,64]{1,0:T(8,128)S(1)} all-reduce(f32[64,64]{1,0:T(8,128)S(1)} %convolution_bitcast_fusion.2), channel_id=1, replica_groups=mesh['tm'=8,'lat'=4,'lon'=8] {'lat','lon'}, use_global_device_ids=true, to_apply=%region_6.7 | all-reduce | flops 4096 | bytes 32768 | tf_op jit(solution)/shard_map/psum | solution.py:132
  (36 shorter events, 2.5 us)
Async XLA Ops:
  7.2 8.8 %copy-start = (bf16[64,8192]{1,0:T(8,128)(2,1)S(1)}, bf16[64,8192]{1,0:T(8,128)(2,1)}, u32[]{:S(2)}) copy-start(bf16[64,8192]{1,0:T(8,128)(2,1)} %param.5) | copy-start | bytes 3145732
  7.2 53.3 %all-gather.9.cloned.1.call-start = ((), (), s32[]{:S(2)}) async-start(), calls=%async_computation.3 | async-start | bytes 2359296 | tf_op jit(solution)/shard_map/all_gather | solution.py:13
  17.2 102.8 %reduce-scatter.2.cloned.1.call-start = ((), (), s32[]{:S(2)}) async-start(), calls=%async_computation.1 | async-start | bytes 2359296 | tf_op jit(solution)/shard_map/reduce_scatter | solution.py:118
  71.9 4.2 %copy-start.1 = (bf16[64,64]{1,0:T(8,128)(2,1)S(1)}, bf16[64,64]{1,0:T(8,128)(2,1)}, u32[]{:S(2)}) copy-start(bf16[64,64]{1,0:T(8,128)(2,1)} %param.6) | copy-start | bytes 24580
  78.0 167.7 %all-gather.7.cloned.1.call-start = ((), (), s32[]{:S(2)}) async-start(), calls=%async_computation.2 | async-start | bytes 1179648 | tf_op jit(solution)/shard_map/all_gather | solution.py:129
Sparse Core Ops, SparseCore 0:
  17.3 43.1 all-gather.8
  78.1 41.8 reduce-scatter.1
  211.0 34.6 all-gather.6
where the time goes:
time: 379 us; the launch traced here: 378 us
  blocking collectives  226 us (60%)
  waiting for transfers between devices  76.9 us (20%)
  between operations  26.8 us (7%)
  matrix products  23.6 us (6%)
  other arithmetic  20 us (5%)
  local copies, waits for them, and re-layouts  4.4 us (1%)
    psum x1, blocking collectives, local(): projections = lax.psum(partial_sums, ('lat', 'lon'))  124 us
    psum x1, blocking collectives, make_orthonormal(): gram_matrix = lax.psum(local_gram_block, ('tm', 'lat', 'lon'))  74.9 us
    reduce_scatter x1, waiting for transfers between devices, local(): lax.psum_scatter(jnp.einsum('tk,tgc->gkc', start, block_of_rows, preferre...  42 us
    all_gather x1, waiting for transfers between devices, local(): lax.all_gather(ortho.astype(jnp.bfloat16), 'tm', axis=0, tiled=True)  34.8 us
    all_gather x1, blocking collectives, prefix(): pieces = jax.tree.map(lambda part: lax.all_gather(part, axis), value)  27.4 us
    dot_general x7, matrix products, combine(): jnp.dot(subsequent[0], earlier[1], precision=TOP_PRECISION) + subsequent[1]  9.15 us
  transfers between devices with their start and end apart: 3, of which 3 were waited for; matrix products, arithmetic and copies ran while one was open for 1% of the time, Pallas kernels for 0%

commit v1 on v0

--- a/solution.py
+++ b/solution.py
@@ -90,7 +90,8 @@
     local_gram_block = jnp.einsum(
         "zrs,zts->rt", spatial_patterns, spatial_patterns, precision=TOP_PRECISION
     )
-    gram_matrix = lax.psum(local_gram_block, ("tm", "lat", "lon"))
+    parts = lax.all_gather(local_gram_block, ("tm", "lat", "lon"))
+    gram_matrix = jnp.sum(parts, axis=0)
     lower_factor = jnp.linalg.cholesky(gram_matrix)
     width = gram_matrix.shape[0]
     inverse_factor = jax.scipy.linalg.solve_triangular(

time: 379 us -> 428 us (1.13)
  waiting for transfers between devices: 76.9 us -> 196 us
  blocking collectives: 226 us -> 151 us
  other arithmetic: 20 us -> 24.3 us
    all_gather x0 -> x1, waiting for transfers between devices: none -> 119 us  [make_orthonormal(): parts = lax.all_gather(local_gram_block, ('tm', 'lat', 'lon'))]
    psum x1 -> x0, blocking collectives: 74.9 us -> none  [make_orthonormal(): gram_matrix = lax.psum(local_gram_block, ('tm', 'lat', 'lon'))]
  transfers between devices with their start and end apart: 3 -> 4, of which waited for: 3 -> 3; matrix products, arithmetic and copies ran while one was open for 1% -> 1% of each run, Pallas kernels for 0% -> 0%
where the time goes in v1:
time: 428 us; the launch traced here: 427 us
  waiting for transfers between devices  196 us (46%)
  blocking collectives  151 us (35%)
  between operations  27 us (6%)
  other arithmetic  24.3 us (6%)
  matrix products  23.3 us (5%)
  local copies, waits for them, and re-layouts  4.33 us (1%)
    psum x1, blocking collectives, local(): projections = lax.psum(partial_sums, ('lat', 'lon'))  124 us
    all_gather x1, waiting for transfers between devices, make_orthonormal(): parts = lax.all_gather(local_gram_block, ('tm', 'lat', 'lon'))  119 us
    reduce_scatter x1, waiting for transfers between devices, local(): lax.psum_scatter(jnp.einsum('tk,tgc->gkc', start, block_of_rows, preferre...  42 us
    all_gather x1, waiting for transfers between devices, local(): lax.all_gather(ortho.astype(jnp.bfloat16), 'tm', axis=0, tiled=True)  35.6 us
    all_gather x1, blocking collectives, prefix(): pieces = jax.tree.map(lambda part: lax.all_gather(part, axis), value)  27.5 us
    dot_general x7, matrix products, combine(): jnp.dot(subsequent[0], earlier[1], precision=TOP_PRECISION) + subsequent[1]  9.15 us
  transfers between devices with their start and end apart: 4, of which 3 were waited for; matrix products, arithmetic and copies ran while one was open for 1% of the time, Pallas kernels for 0%

profile of v1, /device:TPU:32, one launch (start us, length us, event | category | flops | bytes accessed | tf_op | source)
XLA Modules:
  0.0 426.8 jit_solution(18205603155161820418)
XLA Ops:
  7.2 1.0 slice_reduce_fusion
  8.2 1.5 fusion.87
  9.7 0.7 fusion.89
  13.2 1.4 fusion.80
  14.7 1.4 fusion.79
  16.1 1.2 convolution_bitcast_fusion
  28.6 1.4 compare_select_fusion.9
  30.0 1.9 multiply_add_fusion.1
  31.9 1.4 compare_select_fusion.8
  33.3 27.5 %all-gather.3 = f32[8,6,6]{2,1,0:T(8,128)S(1)} all-gather(f32[1,6,6]{2,1,0:T(8,128)S(1)} %bitcast.81), channel_id=2, replica_groups=mesh['tm'=8,'lat'=4,'lon'=8] {'tm'}, dimensions={0}, use_global_device_ids=true | all-gather | bytes 1296 | tf_op jit(solution)/shard_map/all_gather | solution.py:13
  60.8 9.5 %while.14 = (s32[]{:T(128)}, f32[6,8192]{1,0:T(8,128)S(1)}, s32[]{:T(128)}, f32[8,6,6]{2,1,0:T(8,128)S(1)}, f32[8,6,8192]{2,1,0:T(8,128)}, /*index=5*/s32[]{:T(128)}, s32[]{:T(128)}) while((s32[]{:T(128)}, f32[6,8192]{1,0:T(8,128)S(1)}, s32[]{:T(128)}, f32[8,6,6]{2,1,0:T(8,128)S(1)}, f32[8,6,8192]{2,1,0:T(8,128)}, ...), condition=%wide.region_1.2_spmd.clone, body=%wide.region_0.1_spmd.clone.sunk | while | flops 3735556 | bytes 1317479 | solution.py:22
  60.8 1.3 fusion.106
  62.2 1.3 fusion.106
  63.5 1.3 fusion.106
  64.9 1.3 fusion.106
  66.3 1.3 fusion.106
  67.6 1.3 fusion.106
  69.0 1.3 fusion.106
  70.3 1.8 fusion.90
  72.2 4.3 fusion.9
  76.5 1.8 convolution_bitcast_fusion.1
  78.4 42.0 %reduce-scatter.2.cloned.1.call-done = f32[8,64,128]{2,1,0:T(8,128)} async-done(((f32[64,64,128]{2,1,0:T(8,128)}), f32[8,64,128]{2,1,0:T(8,128)}) %reduce-scatter.2.cloned.1.call-update) | async-done | bytes 262160 | tf_op jit(solution)/shard_map/reduce_scatter | solution.py:119
  120.4 2.0 convolution_bitcast_fusion.4
  122.5 118.6 %all-gather.11.cloned.1.call-done = f32[16384,64]{1,0:T(8,128)} async-done(((f32[64,64]{1,0:T(8,128)}), f32[16384,64]{1,0:T(8,128)}) %all-gather.11.cloned.1.call-update) | async-done | bytes 4194320 | tf_op jit(solution)/shard_map/all_gather | solution.py:93
  241.0 4.1 reduce_sum.9
  245.2 5.8 %cholesky.16 = f32[64,64]{1,0:T(8,128)S(1)} custom-call(f32[64,64]{1,0:T(8,128)S(1)} %fusion.16), custom_call_target="Cholesky" | custom-call | tf_op jit(solution)/shard_map/jit(cholesky)/cholesky | solution.py:95
  251.7 0.7 fusion.14
  252.4 4.9 %custom-call.7 = f32[1,64,64]{1,2,0:T(8,128)S(1)} custom-call(f32[1,64,64]{2,1,0:T(8,128)S(1)} %fusion.14), custom_call_target="InvertDiagBlocksLowerTriangular" | custom-call | tf_op jit(solution)/shard_map/jit(_solve_triangular)/triangular_solve | solution.py:97
  257.5 1.1 convert_bitcast_fusion
  258.7 35.6 %all-gather.9.cloned.1.call-done = bf16[64,64,128]{2,1,0:T(8,128)(2,1)} async-done(((bf16[8,64,128]{2,1,0:T(8,128)(2,1)}), bf16[64,64,128]{2,1,0:T(8,128)(2,1)}) %all-gather.9.cloned.1.call-update) | async-done | bytes 1048592 | tf_op jit(solution)/shard_map/all_gather | solution.py:130
  294.3 1.6 convolution_bitcast_fusion.2
  295.9 123.8 %psum.7 = f32[64,64]{1,0:T(8,128)S(1)} all-reduce(f32[64,64]{1,0:T(8,128)S(1)} %convolution_bitcast_fusion.2), channel_id=1, replica_groups=mesh['tm'=8,'lat'=4,'lon'=8] {'lat','lon'}, use_global_device_ids=true, to_apply=%region_6.7 | all-reduce | flops 4096 | bytes 32768 | tf_op jit(solution)/shard_map/psum | solution.py:133
  (41 shorter events, 3.0 us)
Async XLA Ops:
  7.2 8.9 %copy-start = (bf16[64,8192]{1,0:T(8,128)(2,1)S(1)}, bf16[64,8192]{1,0:T(8,128)(2,1)}, u32[]{:S(2)}) copy-start(bf16[64,8192]{1,0:T(8,128)(2,1)} %param.5) | copy-start | bytes 3145732
  7.2 53.6 %all-gather.13.cloned.1.call-start = ((), (), s32[]{:S(2)}) async-start(), calls=%async_computation.4 | async-start | bytes 2359296 | tf_op jit(solution)/shard_map/all_gather | solution.py:13
  17.3 103.1 %reduce-scatter.2.cloned.1.call-start = ((), (), s32[]{:S(2)}) async-start(), calls=%async_computation.1 | async-start | bytes 2359296 | tf_op jit(solution)/shard_map/reduce_scatter | solution.py:119
  72.2 4.3 %copy-start.2 = (bf16[64,64]{1,0:T(8,128)(2,1)S(1)}, bf16[64,64]{1,0:T(8,128)(2,1)}, u32[]{:S(2)}) copy-start(bf16[64,64]{1,0:T(8,128)(2,1)} %param.6) | copy-start | bytes 24580
  78.3 162.7 %all-gather.11.cloned.1.call-start = ((), (), s32[]{:S(2)}) async-start(), calls=%async_computation.3 | async-start | bytes 8421376 | tf_op jit(solution)/shard_map/all_gather | solution.py:93
  122.4 171.8 %all-gather.9.cloned.1.call-start = ((), (), s32[]{:S(2)}) async-start(), calls=%async_computation.2 | async-start | bytes 1179648 | tf_op jit(solution)/shard_map/all_gather | solution.py:130
  241.0 16.5 %copy-start.1 = (f32[8,64,128]{2,1,0:T(8,128)S(1)}, f32[8,64,128]{2,1,0:T(8,128)}, u32[]{:S(2)}) copy-start(f32[8,64,128]{2,1,0:T(8,128)} %reduce-scatter.2.cloned.1.call-done) | copy-start | bytes 786436
Sparse Core Ops, SparseCore 0:
  17.5 42.9 all-gather.12
  78.5 41.8 reduce-scatter.1
  124.7 116.2 all-gather.10
  258.8 35.4 all-gather.8
